TPU v7x, 256 devices: a whole 4x4x8 slice. The times are simulated.
256 devices in a mesh: row: 8 (over z_lo, x), col: 32 (over z_hi, y, core).
Axes of the slice: x: 4, y: 4, z: 8 (z_hi: 4, z_lo: 2; z = z_hi * 2 + z_lo), core: 2. Of those that a mesh axis runs over, the one named last changes fastest.
Arguments:
- image_feats: bfloat16 [3, 56, 224, 1024], P(None, 'row', 'col'), may hold values from -80 to 80
- norm_gain: float32 [1024], replicated, may hold values from 0.5 to 1.5
- w_qkv: bfloat16 [1024, 1536], replicated, may hold values from -0.1875 to 0.1875
- rel_bias: float32 [8, 13, 13], replicated, may hold values from -5 to 355
- w_proj: bfloat16 [512, 1024], replicated, may hold values from -0.25 to 0.25
- out_grad: bfloat16 [3, 56, 224, 1024], P(None, 'row', 'col'), may hold values from -6 to 6
Outputs:
- layer_out: bfloat16 [3, 56, 224, 1024], P(None, 'row', 'col')
- feats_grad: bfloat16 [3, 56, 224, 1024], P(None, 'row', 'col')
- qkv_grad: bfloat16 [1024, 1536], replicated
- proj_grad: bfloat16 [512, 1024], replicated
- gain_grad: float32 [1024], replicated
- bias_grad: float32 [8, 13, 13], replicated
All inputs are finite; a program needn't handle non-finite values.
Results may differ from a plain program's by a relative error of at most 0.017.
Values may be sent and summed in bfloat16 or wider, within the bound.
No kernel may reach another device: no remote copies, remote signals or barrier semaphores. Data moves between devices by JAX's collectives and lax.ppermute only.
A program may use at most 128 MiB of HBM per device.

v0:
```python
import jax
import jax.numpy as jnp
from jax import lax
from jax.sharding import PartitionSpec as P

WIN = 7
norm_eps = 1e-05
highest = lax.Precision.HIGHEST


def shifted(value, axis, steps):
    count = lax.axis_size(axis)
    leading, last = (max(0, -steps), min(count, count - steps))
    return lax.ppermute(value, axis, [(source, source + steps) for source in range(leading, last)])


def with_halo(block, sides, width):
    for axis, dim in sides:
        count = lax.axis_size(axis)
        forward = [(i, i + 1) for i in range(count - 1)]
        backward = [(target, source) for source, target in forward]
        low = lax.ppermute(
            lax.slice_in_dim(block, block.shape[dim] - width, None, axis=dim), axis, forward
        )
        high = lax.ppermute(lax.slice_in_dim(block, 0, width, axis=dim), axis, backward)
        block = jnp.concatenate([low, block, high], axis=dim)
    return block


def window_start(extent, length, anchor):
    position = anchor + jnp.arange(length, dtype=jnp.int32)
    return jnp.clip(position - WIN // 2, 0, extent - WIN)


def return_rims(grad_pad, half_win):
    top_rim = grad_pad[:, :half_win]
    bottom_rim = grad_pad[:, -half_win:]
    from_below = shifted(top_rim.astype(jnp.bfloat16), "row", -1).astype(top_rim.dtype)
    from_above = shifted(bottom_rim.astype(jnp.bfloat16), "row", 1).astype(bottom_rim.dtype)
    middle = grad_pad[:, half_win:-half_win]
    middle = middle.at[:, :half_win].add(from_above)
    middle = middle.at[:, -half_win:].add(from_below)
    left_rim = middle[:, :, :half_win]
    right_rim = middle[:, :, -half_win:]
    from_right = shifted(left_rim.astype(jnp.bfloat16), "col", -1).astype(left_rim.dtype)
    from_left = shifted(right_rim.astype(jnp.bfloat16), "col", 1).astype(right_rim.dtype)
    inner_part = middle[:, :, half_win:-half_win]
    inner_part = inner_part.at[:, :, :half_win].add(from_left)
    inner_part = inner_part.at[:, :, -half_win:].add(from_right)
    return inner_part


def body(image_feats, norm_gain, w_qkv, rel_bias, w_proj, out_grad):
    tile_count, row_count, col_count, model_dim = image_feats.shape
    head_count = rel_bias.shape[0]
    heads_dim = w_proj.shape[0]
    head_size = heads_dim // head_count
    half_win = WIN // 2
    bias_span = rel_bias.shape[1]
    image_height = row_count * lax.axis_size("row")
    image_width = col_count * lax.axis_size("col")
    row_anchor = lax.axis_index("row") * row_count
    col_anchor = lax.axis_index("col") * col_count
    feats_f32 = image_feats.astype(jnp.float32)
    center = jnp.mean(feats_f32, axis=-1, keepdims=True)
    deviation = feats_f32 - center
    spread = jnp.mean(deviation * deviation, axis=-1, keepdims=True)
    inv_std = lax.rsqrt(spread + norm_eps)
    normal_x = deviation * inv_std
    normed = (normal_x * norm_gain).astype(jnp.bfloat16)
    normed_rows = normed.reshape(-1, model_dim)
    qkv_out = jnp.dot(normed_rows, w_qkv, preferred_element_type=jnp.float32).astype(jnp.bfloat16)
    qkv_out = qkv_out.reshape(tile_count, row_count, col_count, 3 * heads_dim)
    patch_count = row_count * col_count
    queries = qkv_out[..., :heads_dim].reshape(tile_count, patch_count, head_count, head_size)
    keys_values = qkv_out[..., heads_dim:]
    padded = with_halo(keys_values, (("row", 1), ("col", 2)), half_win)
    pad_rows = row_count + 2 * half_win
    pad_cols = col_count + 2 * half_win
    key_count = pad_rows * pad_cols
    flat_pad = padded.reshape(tile_count, key_count, 2 * heads_dim)
    pad_keys = flat_pad[..., :heads_dim].reshape(tile_count, key_count, head_count, head_size)
    pad_values = flat_pad[..., heads_dim:].reshape(tile_count, key_count, head_count, head_size)
    row_first = window_start(image_height, row_count, row_anchor) - (row_anchor - half_win)
    col_first = window_start(image_width, col_count, col_anchor) - (col_anchor - half_win)
    pad_row_pos = jnp.arange(pad_rows, dtype=jnp.int32)
    pad_col_pos = jnp.arange(pad_cols, dtype=jnp.int32)
    row_valid = (pad_row_pos[None, :] >= row_first[:, None]) & (
        pad_row_pos[None, :] < row_first[:, None] + WIN
    )
    col_valid = (pad_col_pos[None, :] >= col_first[:, None]) & (
        pad_col_pos[None, :] < col_first[:, None] + WIN
    )
    window_mask = (row_valid[:, None, :, None] & col_valid[None, :, None, :]).reshape(
        patch_count, key_count
    )
    bias_index = jnp.arange(bias_span, dtype=jnp.int32)
    rel_rows = pad_row_pos[None, :] - jnp.arange(row_count, dtype=jnp.int32)[:, None] + half_win
    rel_cols = pad_col_pos[None, :] - jnp.arange(col_count, dtype=jnp.int32)[:, None] + half_win
    row_onehot = (rel_rows[:, :, None] == bias_index[None, None, :]).astype(jnp.float32)
    col_onehot = (rel_cols[:, :, None] == bias_index[None, None, :]).astype(jnp.float32)
    bias_full = jnp.einsum(
        "rkx,hxy,cmy->hrckm", row_onehot, rel_bias, col_onehot, precision=highest
    )
    bias_full = bias_full.reshape(head_count, patch_count, key_count)
    score_scale = head_size ** (-0.5)
    scores = (
        jnp.einsum("bphd,bkhd->bhpk", queries, pad_keys, preferred_element_type=jnp.float32)
        * score_scale
        + bias_full[None]
    )
    scores = jnp.where(window_mask[None, None], scores, -1e30)
    row_peak = jnp.max(scores, axis=-1, keepdims=True)
    exp_terms = jnp.where(window_mask[None, None], jnp.exp(scores - row_peak), 0.0)
    probs_full = exp_terms / jnp.sum(exp_terms, axis=-1, keepdims=True)
    probs_low = probs_full.astype(jnp.bfloat16)
    attended = jnp.einsum(
        "bhpk,bkhd->bphd", probs_low, pad_values, preferred_element_type=jnp.float32
    ).astype(jnp.bfloat16)
    attended_rows = attended.reshape(-1, heads_dim)
    grad_rows = out_grad.reshape(-1, model_dim)
    layer_out = (
        feats_f32
        + jnp.dot(attended_rows, w_proj, preferred_element_type=jnp.float32).reshape(
            feats_f32.shape
        )
    ).astype(jnp.bfloat16)
    attended_grad = jnp.einsum(
        "td,ed->te", grad_rows, w_proj, preferred_element_type=jnp.float32
    ).astype(jnp.bfloat16)
    attn_grad = attended_grad.reshape(tile_count, patch_count, head_count, head_size)
    proj_part = jnp.einsum(
        "te,td->ed", attended_rows, grad_rows, preferred_element_type=jnp.float32
    )
    probs_grad = jnp.einsum(
        "bphd,bkhd->bhpk", attn_grad, pad_values, preferred_element_type=jnp.float32
    )
    inner_sum = jnp.sum(probs_full * probs_grad, axis=-1, keepdims=True)
    score_grad = probs_full * (probs_grad - inner_sum)
    block_grad = jnp.sum(score_grad, axis=0).reshape(
        head_count, row_count, col_count, pad_rows, pad_cols
    )
    score_low = score_grad.astype(jnp.bfloat16)
    query_grad = (
        jnp.einsum("bhpk,bkhd->bphd", score_low, pad_keys, preferred_element_type=jnp.float32)
        * score_scale
    ).astype(jnp.bfloat16)
    query_grad = query_grad.reshape(-1, heads_dim)
    key_pad_grad = (
        jnp.einsum("bhpk,bphd->bkhd", score_low, queries, preferred_element_type=jnp.float32)
        * score_scale
    )
    value_pad_grad = jnp.einsum(
        "bhpk,bphd->bkhd", probs_low, attn_grad, preferred_element_type=jnp.float32
    )
    kv_pad_grad = jnp.concatenate(
        [
            key_pad_grad.reshape(tile_count, key_count, heads_dim),
            value_pad_grad.reshape(tile_count, key_count, heads_dim),
        ],
        axis=-1,
    )
    kv_pad_grad = kv_pad_grad.reshape(tile_count, pad_rows, pad_cols, 2 * heads_dim)
    kv_grad = return_rims(kv_pad_grad, half_win)
    qkv_grad_rows = jnp.concatenate(
        [query_grad, kv_grad.astype(jnp.bfloat16).reshape(-1, 2 * heads_dim)], axis=-1
    )
    qkv_part = jnp.einsum(
        "td,te->de", normed_rows, qkv_grad_rows, preferred_element_type=jnp.float32
    )
    normed_grad = jnp.einsum(
        "te,de->td", qkv_grad_rows, w_qkv, preferred_element_type=jnp.float32
    ).reshape(feats_f32.shape)
    gain_part = jnp.sum(normed_grad * normal_x, axis=(0, 1, 2))
    bias_part = jnp.einsum(
        "rkx,hrckm,cmy->hxy", row_onehot, block_grad, col_onehot, precision=highest
    )
    flat_grads = jnp.concatenate([qkv_part.reshape(-1), proj_part.reshape(-1)])
    grad_share = lax.psum_scatter(flat_grads, ("row", "col"), scatter_dimension=0, tiled=True)
    summed = lax.all_gather(grad_share.astype(jnp.bfloat16), ("row", "col"), axis=0, tiled=True)
    qkv_length = qkv_part.shape[0] * qkv_part.shape[1]
    qkv_grad = summed[:qkv_length].reshape(qkv_part.shape)
    proj_grad = summed[qkv_length:].reshape(proj_part.shape)
    gain_grad, bias_grad = lax.psum((gain_part, bias_part), ("row", "col"))
    scaled = normed_grad * norm_gain
    correction = (
        scaled
        - jnp.mean(scaled, axis=-1, keepdims=True)
        - normal_x * jnp.mean(scaled * normal_x, axis=-1, keepdims=True)
    )
    feats_grad = (out_grad.astype(jnp.float32) + inv_std * correction).astype(jnp.bfloat16)
    return (layer_out, feats_grad, qkv_grad, proj_grad, gain_grad, bias_grad)


def solution(mesh):
    placed = (P(None, "row", "col", None), P(), P(), P(), P(), P(None, "row", "col", None))
    return jax.shard_map(
        body,
        mesh=mesh,
        in_specs=placed,
        out_specs=(P(None, "row", "col", None), P(None, "row", "col", None), P(), P(), P(), P()),
        check_vma=False,
    )
```

profile of v0, /device:TPU:32, one launch (start us, length us, event | category | flops | bytes accessed | tf_op | source)
XLA Modules:
  0.0 768.8 jit_solution(14767202913025241043)
XLA Ops:
  9.8 2.0 fusion.22
  12.8 1.4 convolution_convert_fusion
  14.2 2.0 reshape.375
  16.2 1.7 fusion.61
  17.9 3.4 collective-permute-start
  21.3 4.6 collective-permute-start.1
  25.9 1.8 reshape.380
  28.6 2.5 convolution_convert_fusion.2
  33.6 1.9 reshape.381
  35.5 1.9 reshape.378
  40.9 2.0 collective-permute-start.2
  42.9 1.3 collective-permute-start.3
  44.2 3.2 convolution_bitcast_fusion
  47.3 3.6 reshape.397
  50.9 3.0 pad_maximum_fusion.1
  53.9 2.4 reshape.376
  56.3 2.3 fusion.58
  58.5 2.2 copy.68
  60.7 2.2 copy.67
  62.9 1.7 fusion.7
  64.7 1.5 fusion.62
  66.2 5.2 fusion.14
  71.3 5.6 convolution_bitcast_fusion.2
  77.0 2.4 multiply_reduce_fusion
  81.7 1.6 multiply_bitcast_fusion
  83.3 2.9 copy.43
  86.2 2.8 concatenate.31
  89.0 2.9 copy.41
  91.9 2.8 concatenate.30
  94.7 1.5 constant_dynamic-update-slice_fusion.1
  96.4 1.4 convert.8
  100.3 1.9 reshape.386
  102.1 1.7 copy.39
  103.9 1.9 reshape.382
  105.8 1.7 constant_dynamic-update-slice_fusion.3
  107.4 1.9 fusion.57
  109.3 2.3 collective-permute-start.5
  111.7 3.7 collective-permute-start.4
  115.9 1.8 copy.69
  117.7 3.6 reshape.398
  121.3 3.3 fusion.10
  128.0 3.5 collective-permute-start.6
  135.6 3.4 scatter-add.16
  139.0 2.0 fusion.34
  141.0 1.9 convert_element_type.79
  142.9 1.8 reshape.383
  144.7 1.7 constant_dynamic-update-slice_fusion.2
  146.4 3.1 multiply_reduce_fusion.1
  149.5 3.7 fusion.63
  153.2 2.0 reshape.384
  155.3 1.5 fusion.28
  156.8 6.9 reshape.385
  163.7 6.2 pad_maximum_fusion
  170.0 163.0 %all-reduce.3 = (bf16[2097152]{0:T(1024)(128)(2,1)}, f32[1024]{0:T(1024)}, f32[8,13,13]{2,1,0:T(8,128)}) all-reduce(f32[2097152]{0:T(1024)} %pad_maximum_fusion, f32[1024]{0:T(1024)S(1)} %get-tuple-element.72, f32[8,13,13]{2,1,0:T(8,128)} %convolution_bitcast_fusion.4), channel_id=2, replica_groups=mesh['row'=8,'col'=32] {'row','col'}, use_global_device_ids=true, to_apply=%region_7.8.clone | all-reduce | flops 2099528 | bytes 12601920
  332.9 1.3 dynamic-slice.34
  334.3 1.9 dot_general.58
  336.1 2.5 fusion.8
  338.7 1.5 copy.48
  340.2 2.3 fusion.27
  342.4 405.0 %all-gather.2.cloned.1.call-done = bf16[2097152]{0:T(1024)(128)(2,1)} async-done(((bf16[8192]{0:T(1024)(128)(2,1)}), bf16[2097152]{0:T(1024)(128)(2,1)}) %all-gather.2.cloned.1.call-update) | async-done | bytes 4194320 | tf_op jit(solution)/shard_map/all_gather | solution.py:180
  747.4 3.2 slice.221
  750.6 6.8 reshape.388
  757.4 2.3 slice.222
  759.7 2.3 slice.202
  (73 shorter events, 23.6 us)
Async XLA Ops:
  7.2 5.6 copy-start
  7.2 740.3 %all-gather.2.cloned.1.call-start = ((), (), s32[]{:S(2)}) async-start(), calls=%async_computation | async-start | bytes 4210688 | tf_op jit(solution)/shard_map/all_gather | solution.py:180
  17.9 20.7 %collective-permute-start = (bf16[3,3,7,1024]{3,2,1,0:T(8,128)(2,1)}, bf16[3,3,7,1024]{3,2,1,0:T(8,128)(2,1)}, u32[]{:S(2)}, u32[]{:S(2)}) collective-permute-start(bf16[3,3,7,1024]{3,2,1,0:T(8,128)(2,1)} %get-tuple-element.91), channel_id=1, source_target_pairs={{0,32},{32,64},{64,96},{96,128},{128,160},{160,192},{192,224},{1,3... | collective-permute-start | bytes 387080 | tf_op jit(solution)/shard_map/ppermute | solution.py:22
  21.3 17.3 %collective-permute-start.1 = (bf16[3,3,7,1024]{3,2,1,0:T(8,128)(2,1)}, bf16[3,3,7,1024]{3,2,1,0:T(8,128)(2,1)}, u32[]{:S(2)}, u32[]{:S(2)}) collective-permute-start(bf16[3,3,7,1024]{3,2,1,0:T(8,128)(2,1)} %get-tuple-element.92), channel_id=1, source_target_pairs={{32,0},{64,32},{96,64},{128,96},{160,128},{192,160},{224,192},{33,... | collective-permute-start | bytes 387080 | tf_op jit(solution)/shard_map/ppermute | solution.py:25
  27.7 3.4 copy-start.8
  40.9 10.0 %collective-permute-start.2 = (bf16[3,13,3,1024]{3,2,1,0:T(4,128)(2,1)}, bf16[3,13,3,1024]{3,2,1,0:T(4,128)(2,1)}, u32[]{:S(2)}, u32[]{:S(2)}) collective-permute-start(bf16[3,13,3,1024]{3,2,1,0:T(4,128)(2,1)} %get-tuple-element.89), channel_id=1, source_target_pairs={{0,1},{1,2},{2,3},{3,4},{4,5},{5,6},{6,7},{7,8},{8,9},{9,10},{10,1... | collective-permute-start | bytes 718856 | tf_op jit(solution)/shard_map/ppermute | solution.py:22
  42.9 8.0 %collective-permute-start.3 = (bf16[3,13,3,1024]{3,2,1,0:T(4,128)(2,1)}, bf16[3,13,3,1024]{3,2,1,0:T(4,128)(2,1)}, u32[]{:S(2)}, u32[]{:S(2)}) collective-permute-start(bf16[3,13,3,1024]{3,2,1,0:T(4,128)(2,1)} %get-tuple-element.90), channel_id=1, source_target_pairs={{1,0},{2,1},{3,2},{4,3},{5,4},{6,5},{7,6},{8,7},{9,8},{10,9},{11,1... | collective-permute-start | bytes 718856 | tf_op jit(solution)/shard_map/ppermute | solution.py:25
  64.6 1.5 copy-start.5
  77.0 2.4 copy-start.6
  79.4 1.2 copy-start.4
  80.6 1.1 copy-start.9
  94.7 1.7 copy-start.7
  96.4 1.9 copy-start.2
  98.3 1.2 copy-start.13
  105.8 9.7 %copy-start.10 = (bf16[147,1024]{1,0:T(8,128)(2,1)S(1)}, bf16[147,1024]{1,0:T(8,128)(2,1)}, u32[]{:S(2)}) copy-start(bf16[147,1024]{1,0:T(8,128)(2,1)} %reshape.380) | copy-start | bytes 903172
  105.8 9.7 %copy-start.12 = (bf16[147,512]{1,0:T(8,128)(2,1)S(1)}, bf16[147,512]{1,0:T(8,128)(2,1)}, u32[]{:S(2)}) copy-start(bf16[147,512]{1,0:T(8,128)(2,1)} %reshape.386) | copy-start | bytes 451588
  109.3 16.6 %collective-permute-start.5 = (bf16[3,3,13,1024]{3,2,1,0:T(8,128)(2,1)}, bf16[3,3,13,1024]{3,2,1,0:T(8,128)(2,1)}, u32[]{:S(2)}, u32[]{:S(2)}) collective-permute-start(bf16[3,3,13,1024]{3,2,1,0:T(8,128)(2,1)} %get-tuple-element.83), channel_id=1, source_target_pairs={{32,0},{64,32},{96,64},{128,96},{160,128},{192,160},{224,192},{33,... | collective-permute-start | bytes 718856 | tf_op jit(solution)/shard_map/ppermute | solution.py:14
  111.7 13.1 %collective-permute-start.4 = (bf16[3,3,13,1024]{3,2,1,0:T(8,128)(2,1)}, bf16[3,3,13,1024]{3,2,1,0:T(8,128)(2,1)}, u32[]{:S(2)}, u32[]{:S(2)}) collective-permute-start(bf16[3,3,13,1024]{3,2,1,0:T(8,128)(2,1)} %get-tuple-element.84), channel_id=1, source_target_pairs={{0,32},{32,64},{64,96},{96,128},{128,160},{160,192},{192,224},{1,3... | collective-permute-start | bytes 718856 | tf_op jit(solution)/shard_map/ppermute | solution.py:14
  121.3 3.5 copy-start.1
  128.0 6.7 collective-permute-start.6
  133.4 5.6 collective-permute-start.7
  139.0 7.4 copy-start.14
  146.4 3.1 copy-start.11
  153.2 2.1 copy-start.3
Sparse Core Ops, SparseCore 0:
  334.4 413.0 all-gather.1
where the time goes:
time: 771 us; the launch traced here: 769 us
  waiting for transfers between devices  405 us (53%)
  blocking collectives  163 us (21%)
  local copies, waits for them, and re-layouts  93.5 us (12%)
  matrix products  39.9 us (5%)
  other arithmetic  31 us (4%)
  starting transfers between devices  22.1 us (3%)
  between operations  14.3 us (2%)
    all_gather x1, waiting for transfers between devices, body(): lax.all_gather(grad_share.astype(jnp.bfloat16), ('row', 'col'), axis=0, t...  405 us
    unnamed x1, blocking collectives  163 us
  transfers between devices with their start and end apart: 9, of which 2 were waited for; matrix products, arithmetic and copies ran while one was open for 6% of the time, Pallas kernels for 0%

commit v1 on v0

--- a/solution.py
+++ b/solution.py
@@ -2,6 +2,7 @@
 import jax.numpy as jnp
 from jax import lax
 from jax.sharding import PartitionSpec as P
+from jax.lax import all_to_all, axis_size
 
 WIN = 7
 norm_eps = 1e-05
@@ -177,7 +178,15 @@
     )
     flat_grads = jnp.concatenate([qkv_part.reshape(-1), proj_part.reshape(-1)])
     grad_share = lax.psum_scatter(flat_grads, ("row", "col"), scatter_dimension=0, tiled=True)
-    summed = lax.all_gather(grad_share.astype(jnp.bfloat16), ("row", "col"), axis=0, tiled=True)
+    summed = jnp.concatenate(
+        all_to_all(
+            jnp.stack([grad_share.astype(jnp.bfloat16)] * axis_size(("row", "col"))),
+            axis_name=("row", "col"),
+            split_axis=0,
+            concat_axis=0,
+        ),
+        0,
+    )
     qkv_length = qkv_part.shape[0] * qkv_part.shape[1]
     qkv_grad = summed[:qkv_length].reshape(qkv_part.shape)
     proj_grad = summed[qkv_length:].reshape(proj_part.shape)

time: 771 us -> 545 us (0.71)
  waiting for transfers between devices: 405 us -> 92.7 us
  local copies, waits for them, and re-layouts: 93.5 us -> 155 us
  other arithmetic: 31 us -> 56.4 us
  between operations: 14.3 us -> 1.2 us
  starting transfers between devices: 22.1 us -> 30.8 us
    all_gather x1 -> x0, waiting for transfers between devices: 405 us -> none  [body(): lax.all_gather(grad_share.astype(jnp.bfloat16), ('row', 'col'), axis=0, t...]
    all_to_all x0 -> x1, waiting for transfers between devices: none -> 92.7 us  [body(): all_to_all(jnp.stack([grad_share.astype(jnp.bfloat16)] * axis_size(('row'...]
    unnamed x37 -> x51, local copies, waits for them, and re-layouts: 12.9 us -> 46.7 us
    another operation x2 -> x3, other arithmetic: 1.51 us -> 28.4 us  [the longest x1 26.9 us: body(): jnp.stack([grad_share.astype(jnp.bfloat16)] * axis_size(('row', 'col')))]
    slice x1, local copies, waits for them, and re-layouts: 3.19 us -> 21.3 us  [body(): qkv_grad = summed[:qkv_length].reshape(qkv_part.shape)]
    all_to_all x0 -> x1, starting transfers between devices: none -> 8.75 us  [body(): all_to_all(jnp.stack([grad_share.astype(jnp.bfloat16)] * axis_size(('row'...]
  transfers between devices with their start and end apart: 9 -> 9, of which waited for: 2 -> 2; matrix products, arithmetic and copies ran while one was open for 6% -> 7% of each run, Pallas kernels for 0% -> 0%
where the time goes in v1:
time: 545 us; the launch traced here: 536 us
  blocking collectives  162 us (30%)
  local copies, waits for them, and re-layouts  155 us (28%)
  waiting for transfers between devices  92.7 us (17%)
  other arithmetic  56.4 us (10%)
  matrix products  37.9 us (7%)
  starting transfers between devices  30.8 us (6%)
    unnamed x1, blocking collectives  162 us
    all_to_all x1, waiting for transfers between devices, body(): all_to_all(jnp.stack([grad_share.astype(jnp.bfloat16)] * axis_size(('row'...  92.7 us
    unnamed x51, local copies, waits for them, and re-layouts  46.7 us
    another operation x1, other arithmetic, body(): jnp.stack([grad_share.astype(jnp.bfloat16)] * axis_size(('row', 'col')))  26.9 us
    slice x1, local copies, waits for them, and re-layouts, body(): qkv_grad = summed[:qkv_length].reshape(qkv_part.shape)  21.3 us
  transfers between devices with their start and end apart: 9, of which 2 were waited for; matrix products, arithmetic and copies ran while one was open for 7% of the time, Pallas kernels for 0%

profile of v1, /device:TPU:32, one launch (start us, length us, event | category | flops | bytes accessed | tf_op | source)
XLA Modules:
  0.0 536.3 jit_solution(17094045198356224967)
XLA Ops:
  0.6 1.3 convert_reduce_fusion
  3.2 2.0 fusion.17
  6.2 1.4 convolution_convert_fusion
  7.7 2.0 reshape.385
  9.6 1.7 fusion.55
  11.3 3.4 collective-permute-start
  14.7 4.6 collective-permute-start.1
  19.3 1.8 reshape.390
  22.0 2.5 convolution_convert_fusion.2
  27.1 1.9 reshape.391
  28.9 1.9 reshape.388
  34.3 2.0 collective-permute-start.2
  36.3 1.3 collective-permute-start.3
  37.6 3.2 convolution_bitcast_fusion
  40.8 4.0 reshape.408
  44.8 3.0 pad_maximum_fusion.1
  47.8 2.4 reshape.386
  50.2 2.3 fusion.52
  52.4 2.2 copy.86
  54.6 2.2 copy.85
  56.8 1.7 fusion.5
  58.6 1.5 fusion.56
  60.1 5.2 fusion.9
  65.3 5.6 %convolution_bitcast_fusion.2 = f32[3,169,8,64]{1,3,2,0:T(8,128)} fusion(bf16[3,49,8,64]{3,2,1,0:T(8,128)(2,1)} %reshape.391, f32[3,8,49]{2,1,0:T(8,128)S(1)} %get-tuple-element.99, f32[3,8,49,169]{3,2,1,0:T(8,128)} %copy-done.7, pred[49,169]{1,0:T(8,128)(4,1)S(1)} %and.53), kind=kOutput, calls=%fused_computation.9 | convolution fusion | flops 26235552 | bytes 1996825 | tf_op jit(solution)/shard_map/bhpk,bphd->bkhd/dot_general | solution.py:154
  70.9 2.4 multiply_reduce_fusion
  75.6 1.6 multiply_bitcast_fusion
  77.2 2.9 copy.61
  80.1 2.7 concatenate.31
  82.8 2.9 copy.59
  85.7 2.8 concatenate.30
  88.5 1.5 constant_dynamic-update-slice_fusion.1
  90.3 1.4 convert.8
  94.1 1.9 reshape.396
  96.0 1.7 copy.57
  97.7 1.9 reshape.392
  99.6 1.6 constant_dynamic-update-slice_fusion.3
  101.3 1.9 fusion.51
  103.2 2.3 collective-permute-start.5
  105.4 3.8 collective-permute-start.4
  109.7 1.8 copy.87
  111.5 3.6 reshape.409
  115.1 3.3 convolution_bitcast_fusion.3
  121.8 3.5 collective-permute-start.6
  126.6 1.3 collective-permute-start.7
  128.8 3.4 scatter-add.16
  132.2 2.0 fusion.29
  134.2 1.9 convert_element_type.79
  136.1 1.8 reshape.393
  137.9 1.7 constant_dynamic-update-slice_fusion.2
  139.6 3.1 multiply_reduce_fusion.1
  142.7 3.7 fusion.57
  147.8 7.1 %reshape.395 = f32[1572864]{0:T(1024)} reshape(f32[1024,1536]{1,0:T(8,128)} %fusion.57) | data formatting | bytes 12582912 | tf_op jit(solution)/shard_map/reshape | solution.py:179
  154.9 7.1 %pad_maximum_fusion = f32[2097152]{0:T(1024)} fusion(f32[524288]{0:T(1024)S(1)} %bitcast.82, f32[1572864]{0:T(1024)} %reshape.395), kind=kLoop, calls=%fused_computation.1 | loop fusion | flops 2097152 | bytes 16777216 | tf_op jit(solution)/shard_map/concatenate | solution.py:179
  162.1 162.2 %all-reduce.3 = (bf16[2097152]{0:T(1024)(128)(2,1)}, f32[1024]{0:T(1024)}, f32[8,13,13]{2,1,0:T(8,128)S(1)}) all-reduce(f32[2097152]{0:T(1024)} %pad_maximum_fusion, f32[1024]{0:T(1024)S(1)} %get-tuple-element.78, f32[8,13,13]{2,1,0:T(8,128)S(1)} %convolution_bitcast_fusion.5), channel_id=2, replica_groups=mesh['row'=8,'col'=32] {'row','col'}, use_global_device_ids=true, to_apply=%region_7.8.clone | all-reduce | flops 2099528 | bytes 12601920
  325.0 5.5 %stack.2 = bf16[256,1,8192]{2,1,0:T(2,128)(2,1)} broadcast(bf16[8192]{0:T(1024)(128)(2,1)S(1)} %dynamic-slice.34), dimensions={2} | broadcast | bytes 4210688 | tf_op jit(solution)/shard_map/stack | solution.py:183
  331.0 26.9 %reduce.13 = bf16[256,8192]{1,0:T(8,128)(2,1)} reduce(bf16[256,1,8192]{2,1,0:T(2,128)(2,1)} %stack.2, bf16[]{:T(256)} %broadcast.297), dimensions={1}, to_apply=%stack.2.reduce_sub_computation | reduce | bytes 8388610 | tf_op jit(solution)/shard_map/stack | solution.py:183
  357.9 7.8 %reshape.412 = bf16[256,2,4096]{2,1,0:T(2,128)(2,1)} reshape(bf16[256,8192]{1,0:T(8,128)(2,1)} %reduce.13) | data formatting | bytes 8388608
  365.7 8.7 %all-to-all-start = ((bf16[256,2,4096]{2,1,0:T(2,128)(2,1)}), bf16[256,2,4096]{2,1,0:T(2,128)(2,1)}, u32[]{:S(2)}, u32[]{:S(2)}) async-start(bf16[256,2,4096]{2,1,0:T(2,128)(2,1)} %reshape.412), calls=%async_computation | async-start | bytes 8388608 | tf_op jit(solution)/shard_map/all_to_all | solution.py:182
  377.7 92.7 %all-to-all-done = bf16[256,2,4096]{2,1,0:T(2,128)(2,1)} async-done(((bf16[256,2,4096]{2,1,0:T(2,128)(2,1)}), bf16[256,2,4096]{2,1,0:T(2,128)(2,1)}, u32[]{:S(2)}, u32[]{:S(2)}) %all-to-all-start) | async-done | bytes 4194336 | tf_op jit(solution)/shard_map/all_to_all | solution.py:182
  470.3 26.6 %reshape.413 = bf16[256,1,8192]{2,1,0:T(2,128)(2,1)} reshape(bf16[256,2,4096]{2,1,0:T(2,128)(2,1)} %all-to-all-done) | data formatting | bytes 8388608
  496.9 8.9 %slice_reduce_fusion.1 = bf16[64,8192]{1,0:T(8,128)(2,1)} fusion(bf16[256,1,8192]{2,1,0:T(2,128)(2,1)} %reshape.413), kind=kLoop, calls=%fused_computation.4 | loop fusion | bytes 2097152 | tf_op jit(solution)/shard_map/slice | solution.py:192
  505.8 21.3 %slice_reduce_fusion = bf16[192,8192]{1,0:T(8,128)(2,1)} fusion(bf16[256,1,8192]{2,1,0:T(2,128)(2,1)} %reshape.413), kind=kLoop, calls=%fused_computation.2 | loop fusion | bytes 6291456 | tf_op jit(solution)/shard_map/slice | solution.py:191
  527.1 6.7 %reshape.398 = bf16[1024,1536]{1,0:T(8,128)(2,1)} reshape(bf16[192,8192]{1,0:T(8,128)(2,1)} %slice_reduce_fusion) | data formatting | bytes 6291456 | tf_op jit(solution)/shard_map/reshape | solution.py:191
  533.7 2.3 reshape.399
  (89 shorter events, 26.1 us)
Async XLA Ops:
  0.6 5.6 %copy-start = (bf16[1024,1536]{1,0:T(8,128)(2,1)S(1)}, bf16[1024,1536]{1,0:T(8,128)(2,1)}, u32[]{:S(2)}) copy-start(bf16[1024,1536]{1,0:T(8,128)(2,1)} %param.16) | copy-start | bytes 9437188
  11.3 20.7 %collective-permute-start = (bf16[3,3,7,1024]{3,2,1,0:T(8,128)(2,1)}, bf16[3,3,7,1024]{3,2,1,0:T(8,128)(2,1)}, u32[]{:S(2)}, u32[]{:S(2)}) collective-permute-start(bf16[3,3,7,1024]{3,2,1,0:T(8,128)(2,1)} %get-tuple-element.97), channel_id=1, source_target_pairs={{0,32},{32,64},{64,96},{96,128},{128,160},{160,192},{192,224},{1,3... | collective-permute-start | bytes 387080 | tf_op jit(solution)/shard_map/ppermute | solution.py:23
  14.7 17.3 %collective-permute-start.1 = (bf16[3,3,7,1024]{3,2,1,0:T(8,128)(2,1)}, bf16[3,3,7,1024]{3,2,1,0:T(8,128)(2,1)}, u32[]{:S(2)}, u32[]{:S(2)}) collective-permute-start(bf16[3,3,7,1024]{3,2,1,0:T(8,128)(2,1)} %get-tuple-element.98), channel_id=1, source_target_pairs={{32,0},{64,32},{96,64},{128,96},{160,128},{192,160},{224,192},{33,... | collective-permute-start | bytes 387080 | tf_op jit(solution)/shard_map/ppermute | solution.py:26
  21.1 3.4 copy-start.11
  34.3 10.5 %collective-permute-start.2 = (bf16[3,13,3,1024]{3,2,1,0:T(4,128)(2,1)}, bf16[3,13,3,1024]{3,2,1,0:T(4,128)(2,1)}, u32[]{:S(2)}, u32[]{:S(2)}) collective-permute-start(bf16[3,13,3,1024]{3,2,1,0:T(4,128)(2,1)} %get-tuple-element.95), channel_id=1, source_target_pairs={{0,1},{1,2},{2,3},{3,4},{4,5},{5,6},{6,7},{7,8},{8,9},{9,10},{10,1... | collective-permute-start | bytes 718856 | tf_op jit(solution)/shard_map/ppermute | solution.py:23
  36.3 8.5 %collective-permute-start.3 = (bf16[3,13,3,1024]{3,2,1,0:T(4,128)(2,1)}, bf16[3,13,3,1024]{3,2,1,0:T(4,128)(2,1)}, u32[]{:S(2)}, u32[]{:S(2)}) collective-permute-start(bf16[3,13,3,1024]{3,2,1,0:T(4,128)(2,1)} %get-tuple-element.96), channel_id=1, source_target_pairs={{1,0},{2,1},{3,2},{4,3},{5,4},{6,5},{7,6},{8,7},{9,8},{10,9},{11,1... | collective-permute-start | bytes 718856 | tf_op jit(solution)/shard_map/ppermute | solution.py:26
  58.6 1.5 copy-start.7
  70.9 2.4 copy-start.8
  73.2 1.2 copy-start.6
  74.5 1.1 copy-start.12
  88.5 1.7 copy-start.9
  90.3 1.9 copy-start.3
  92.2 1.2 copy-start.19
  99.6 9.6 %copy-start.13 = (bf16[147,1024]{1,0:T(8,128)(2,1)S(1)}, bf16[147,1024]{1,0:T(8,128)(2,1)}, u32[]{:S(2)}) copy-start(bf16[147,1024]{1,0:T(8,128)(2,1)} %reshape.390) | copy-start | bytes 903172
  99.6 9.6 %copy-start.18 = (bf16[147,512]{1,0:T(8,128)(2,1)S(1)}, bf16[147,512]{1,0:T(8,128)(2,1)}, u32[]{:S(2)}) copy-start(bf16[147,512]{1,0:T(8,128)(2,1)} %reshape.396) | copy-start | bytes 451588
  103.2 16.6 %collective-permute-start.5 = (bf16[3,3,13,1024]{3,2,1,0:T(8,128)(2,1)}, bf16[3,3,13,1024]{3,2,1,0:T(8,128)(2,1)}, u32[]{:S(2)}, u32[]{:S(2)}) collective-permute-start(bf16[3,3,13,1024]{3,2,1,0:T(8,128)(2,1)} %get-tuple-element.89), channel_id=1, source_target_pairs={{32,0},{64,32},{96,64},{128,96},{160,128},{192,160},{224,192},{33,... | collective-permute-start | bytes 718856 | tf_op jit(solution)/shard_map/ppermute | solution.py:15
  105.4 13.1 %collective-permute-start.4 = (bf16[3,3,13,1024]{3,2,1,0:T(8,128)(2,1)}, bf16[3,3,13,1024]{3,2,1,0:T(8,128)(2,1)}, u32[]{:S(2)}, u32[]{:S(2)}) collective-permute-start(bf16[3,3,13,1024]{3,2,1,0:T(8,128)(2,1)} %get-tuple-element.90), channel_id=1, source_target_pairs={{0,32},{32,64},{64,96},{96,128},{128,160},{160,192},{192,224},{1,3... | collective-permute-start | bytes 718856 | tf_op jit(solution)/shard_map/ppermute | solution.py:15
  115.1 3.4 copy-start.2
  121.8 6.1 %collective-permute-start.6 = (bf16[3,7,3,1024]{3,2,1,0:T(4,128)(2,1)S(1)}, bf16[3,7,3,1024]{3,2,1,0:T(4,128)(2,1)S(1)}, u32[]{:S(2)}, u32[]{:S(2)}) collective-permute-start(bf16[3,7,3,1024]{3,2,1,0:T(4,128)(2,1)S(1)} %get-tuple-element.94), channel_id=1, source_target_pairs={{0,1},{1,2},{2,3},{3,4},{4,5},{5,6},{6,7},{7,8},{8,9},{9,10},{10,1... | collective-permute-start | bytes 387080 | tf_op jit(solution)/shard_map/ppermute | solution.py:15
  126.6 5.6 %collective-permute-start.7 = (bf16[3,7,3,1024]{3,2,1,0:T(4,128)(2,1)}, bf16[3,7,3,1024]{3,2,1,0:T(4,128)(2,1)}, u32[]{:S(2)}, u32[]{:S(2)}) collective-permute-start(bf16[3,7,3,1024]{3,2,1,0:T(4,128)(2,1)} %get-tuple-element.93), channel_id=1, source_target_pairs={{1,0},{2,1},{3,2},{4,3},{5,4},{6,5},{7,6},{8,7},{9,8},{10,9},{11,1... | collective-permute-start | bytes 387080 | tf_op jit(solution)/shard_map/ppermute | solution.py:15
  132.2 7.4 %copy-start.20 = (f32[1024]{0:T(1024)S(1)}, f32[1024]{0:T(1024)}, u32[]{:S(2)}) copy-start(f32[1024]{0:T(1024)} %param.15) | copy-start | bytes 12292
  139.6 3.1 copy-start.15
  142.7 3.7 copy-start.16
  146.4 1.0 copy-start.4
  147.8 7.1 %copy-start.5 = (f32[64,8,8,128]{3,1,2,0:T(8,128)S(1)}, f32[64,8,8,128]{3,1,2,0:T(8,128)}, u32[]{:S(2)}) copy-start(f32[64,8,8,128]{3,1,2,0:T(8,128)} %copy.87) | copy-start | bytes 6291460
  365.7 8.8 %copy-start.14 = (bf16[3,49,8,64]{3,2,1,0:T(8,128)(2,1)S(1)}, bf16[3,49,8,64]{3,2,1,0:T(8,128)(2,1)}, u32[]{:S(2)}) copy-start(bf16[3,49,8,64]{3,2,1,0:T(8,128)(2,1)} %copy.55) | copy-start | bytes 451588
  365.7 9.0 %copy-start.10 = (bf16[512,1024]{1,0:T(8,128)(2,1)S(1)}, bf16[512,1024]{1,0:T(8,128)(2,1)}, u32[]{:S(2)}) copy-start(bf16[512,1024]{1,0:T(8,128)(2,1)} %param.18) | copy-start | bytes 3145732
  365.7 104.6 %all-to-all-start = ((bf16[256,2,4096]{2,1,0:T(2,128)(2,1)}), bf16[256,2,4096]{2,1,0:T(2,128)(2,1)}, u32[]{:S(2)}, u32[]{:S(2)}) async-start(bf16[256,2,4096]{2,1,0:T(2,128)(2,1)} %reshape.412), calls=%async_computation | async-start | bytes 8388608 | tf_op jit(solution)/shard_map/all_to_all | solution.py:182
  374.5 2.1 copy-start.17
  527.1 9.0 %copy-start.1 = (bf16[1024,1536]{1,0:T(8,128)(2,1)S(1)}, bf16[1024,1536]{1,0:T(8,128)(2,1)}, u32[]{:S(2)}) copy-start(bf16[1024,1536]{1,0:T(8,128)(2,1)} %param.16) | copy-start | bytes 9437188
